TPU v7x, 32 devices: a whole 2x2x4 slice. The times are simulated.
32 devices in a mesh: parts: 2 (over y), slab: 4 (over z), orb: 2 (over x), pen: 2 (over core).
Axes of the slice: x: 2, y: 2, z: 4, core: 2. Of those that a mesh axis runs over, the one named last changes fastest.
Arguments:
- orbitals: float32 [128, 16, 8, 256], P(('parts', 'orb'), 'slab', 'pen'), parts along dimension 0, may hold values from -7.6 to 7.6
- energies: float32 [128], P(('parts', 'orb')), parts along dimension 0, may hold values from -1 to 0.5
- frequency: float32 [2], P('parts'), parts along dimension 0, may hold values from 0.5 to 2
- local_potential: float32 [16, 8, 256], P('slab', 'pen'), may hold values from -1 to 1
- perturbation: float32 [16, 8, 256], P('slab', 'pen'), may hold values from 0.5 to 1.5
- projectors: float32 [128, 8, 256], P(None, 'pen'), may hold values from -0.0625 to 0.0625
- profiles: float32 [128, 5], replicated, may hold values from 0.5 to 2
- couplings: float32 [128], replicated, may hold values from 4 to 12
- atom_planes: int32 [128], replicated, may hold values from 0 to 15
Outputs:
- response_real: float32 [128, 16, 8, 256], P(('parts', 'orb'), 'slab', 'pen'), parts along dimension 0
- density: float32 [32, 8, 256], P(('parts', 'slab'), 'pen'), parts along dimension 0
There are 2 independent parts, one for each index of `parts`. A program takes and returns all parts, laid end to end along the dimension named above; an argument that names none is the same for every part. Nothing has to cross between parts.
Inputs may be any that keep to these rules, and one draw needn't show every extreme that they name: Projector a covers the planes (atom_planes[a] + d) mod 16 of the first dimension for d < 5.
All inputs are finite; a program needn't handle non-finite values.
Results may differ from a plain program's by a relative error of at most 0.0003.
Values sent between devices are 32-bit elements; how exact they have to be, the bound alone decides.
A program may use at most 64 MiB of HBM per device.

v0:
```python
import jax
import jax.numpy as jnp
from jax import lax
from jax.sharding import PartitionSpec as P

NOCC = 64
ITERS = 2
kinetic_scale = 0.125
highest = lax.Precision.HIGHEST


def extended(cells, sides, width):
    for axis, dim in sides:
        count = lax.axis_size(axis)
        head = lax.slice_in_dim(cells, 0, width, axis=dim)
        tail = lax.slice_in_dim(cells, cells.shape[dim] - width, cells.shape[dim], axis=dim)
        cells = jnp.concatenate(
            [
                lax.ppermute(tail, axis, [(i, (i + 1) % count) for i in range(count)]),
                cells,
                lax.ppermute(head, axis, [((i + 1) % count, i) for i in range(count)]),
            ],
            axis=dim,
        )
    return cells


def plane_weights(atom_planes, profiles, planes, depth_total):
    span_size = profiles.shape[1]
    covered = (atom_planes[:, None] + jnp.arange(span_size, dtype=jnp.int32)[None, :]) % depth_total
    matches = (covered[:, :, None] == planes[None, None, :]).astype(jnp.float32)
    return jnp.sum(profiles[:, :, None] * matches, axis=1)


def coefficients(values, projectors, weights, couplings):
    orb_count, plane_count, row_count, col_count = values.shape
    flat_values = values.reshape(orb_count * plane_count, row_count * col_count)
    flat_beta = projectors.reshape(projectors.shape[0], row_count * col_count)
    inner_sums = lax.dot_general(
        flat_beta, flat_values, (((1,), (1,)), ((), ())), precision=highest
    )
    inner_sums = inner_sums.reshape(projectors.shape[0], orb_count, plane_count)
    partial_sum = jnp.einsum("aiz,az->ai", inner_sums, weights, precision=highest)
    summed = lax.psum(partial_sum, ("slab", "pen"))
    return couplings[:, None] * summed


def apply_section(padded, potential, beta_out, weights_out, expansion, energies):
    centre = padded[:, 1:-1, 1:-1]
    beside_all = (
        padded[:, 2:, 1:-1] + padded[:, :-2, 1:-1] + padded[:, 1:-1, 2:] + padded[:, 1:-1, :-2]
    )
    beside_all = beside_all + jnp.roll(centre, 1, 3) + jnp.roll(centre, -1, 3)
    orb_count, plane_count, row_count, col_count = centre.shape
    spread = weights_out[:, None, :] * expansion[:, :, None]
    flat_spread = spread.reshape(spread.shape[0], orb_count * plane_count)
    flat_beta = beta_out.reshape(beta_out.shape[0], row_count * col_count)
    nonlocal_term = lax.dot_general(
        flat_spread, flat_beta, (((0,), (0,)), ((), ())), precision=highest
    )
    nonlocal_term = nonlocal_term.reshape(orb_count, plane_count, row_count, col_count)
    return (
        kinetic_scale * (6.0 * centre - beside_all)
        + potential[None] * centre
        + nonlocal_term
        - energies[:, None, None, None] * centre
    )


def on_device(
    orbitals,
    energies,
    frequency,
    local_potential,
    perturbation,
    projectors,
    profiles,
    couplings,
    atom_planes,
):
    orb_count, plane_count, row_count, col_count = orbitals.shape
    depth_total = plane_count * lax.axis_size("slab")
    cell_total = float(depth_total * row_count * lax.axis_size("pen") * col_count)
    first_plane = lax.axis_index("slab") * plane_count
    planes = (first_plane + jnp.arange(plane_count, dtype=jnp.int32)) % depth_total
    weights = plane_weights(atom_planes, profiles, planes, depth_total)
    freq_square = frequency[0] * frequency[0]
    everyone = lax.all_gather(orbitals, "orb", axis=0, tiled=True)
    every_flat = everyone.reshape(everyone.shape[0], -1)

    def correlation_terms(values):
        return lax.dot_general(
            every_flat, values.reshape(orb_count, -1), (((1,), (1,)), ((), ())), precision=highest
        )

    def removed(values, totals, factor):
        expansion = jax.scipy.linalg.cho_solve((factor, True), totals / cell_total)
        removed_part = lax.dot_general(
            expansion, every_flat, (((0,), (0,)), ((), ())), precision=highest
        )
        return values - removed_part.reshape(values.shape)

    def squares(values):
        return lax.psum(jnp.sum(values * values, axis=(1, 2, 3)), ("slab", "pen"))

    def apply_shallow(values):
        padded = extended(values, (("slab", 1), ("pen", 2)), 1)
        expansion = coefficients(values, projectors, weights, couplings)
        return apply_section(padded, local_potential, projectors, weights, expansion, energies)

    source = perturbation[None] * orbitals
    gram_part = lax.dot_general(every_flat, every_flat, (((1,), (1,)), ((), ())), precision=highest)
    gram_total, source_total = lax.psum((gram_part, correlation_terms(source)), ("slab", "pen"))
    factor = jnp.linalg.cholesky(gram_total / cell_total)
    residual = -removed(source, source_total, factor)
    direction = residual
    solution = jnp.zeros_like(residual)
    norm_now = squares(residual)
    for iteration in range(ITERS):
        direction_total = lax.psum(correlation_terms(direction), ("slab", "pen"))
        inner_field = removed(direction, direction_total, factor)
        first_half = apply_shallow(inner_field)
        second = apply_shallow(first_half)
        first_half, second = (first_half, second)
        target = second + freq_square * inner_field
        curve_part = jnp.sum(first_half * first_half, axis=(1, 2, 3)) + freq_square * jnp.sum(
            inner_field * inner_field, axis=(1, 2, 3)
        )
        image_total, curvature = lax.psum((correlation_terms(target), curve_part), ("slab", "pen"))
        image_field = removed(target, image_total, factor)
        step_size = norm_now / curvature
        solution = solution + step_size[:, None, None, None] * direction
        residual = residual - step_size[:, None, None, None] * image_field
        norm_next = squares(residual)
        direction = residual + (norm_next / norm_now)[:, None, None, None] * direction
        norm_now = norm_next
    padded = extended(solution, (("slab", 1), ("pen", 2)), 1)
    final_expansion = coefficients(solution, projectors, weights, couplings)
    response_real = apply_section(
        padded, local_potential, projectors, weights, final_expansion, energies
    )
    density = lax.psum(jnp.sum(orbitals * response_real, axis=0), "orb") * (4.0 / NOCC)
    return (response_real, density)


def solution(mesh):
    in_specs = (
        P(("parts", "orb"), "slab", "pen", None),
        P(("parts", "orb")),
        P("parts"),
        P("slab", "pen", None),
        P("slab", "pen", None),
        P(None, "pen", None),
        P(),
        P(),
        P(),
    )
    out_specs = (P(("parts", "orb"), "slab", "pen", None), P(("parts", "slab"), "pen", None))
    return jax.shard_map(
        on_device, mesh=mesh, in_specs=in_specs, out_specs=out_specs, check_vma=False
    )
```

profile of v0, /device:TPU:0, one launch (start us, length us, event | category | flops | bytes accessed | tf_op | source)
XLA Modules:
  0.0 372.5 jit_solution(15849839324657514728)
XLA Ops:
  7.2 2.1 copy.40
  10.5 1.0 copy.48
  12.3 21.8 %all-gather.2.cloned.1.call-done = f32[64,4,4,256]{3,0,2,1:T(8,128)} async-done(((f32[32,4,4,256]{3,0,2,1:T(8,128)}), f32[64,4,4,256]{3,0,2,1:T(8,128)}) %all-gather.2.cloned.1.call-update) | async-done | bytes 1048592 | tf_op jit(solution)/shard_map/all_gather | solution.py:88
  34.1 2.6 convolution_bitcast_fusion
  36.8 1.1 convolution_bitcast_fusion.4
  37.9 28.8 %all-reduce.1 = (f32[64,64]{0,1:T(8,128)S(1)}, f32[64,32]{0,1:T(8,128)S(1)}) all-reduce(f32[64,64]{0,1:T(8,128)S(1)} %convolution_bitcast_fusion, f32[64,32]{0,1:T(8,128)S(1)} %convolution_bitcast_fusion.4), channel_id=1, replica_groups=mesh['parts'=2,'slab'=4,'orb'=2,'pen'=2] {'slab','pen'}, use_global_device_ids=true, to_apply=%region_0.1 | all-reduce | flops 6144 | bytes 49152 | tf_op jit(solution)/shard_map/psum | solution.py:113
  66.8 5.8 %cholesky.18 = f32[64,64]{1,0:T(8,128)S(1)} custom-call(f32[64,64]{1,0:T(8,128)S(1)} %fusion.65), custom_call_target="Cholesky" | custom-call | tf_op jit(solution)/shard_map/jit(cholesky)/cholesky | solution.py:114
  74.0 4.9 %custom-call.11 = f32[1,64,64]{1,2,0:T(8,128)S(1)} custom-call(f32[1,64,64]{2,1,0:T(8,128)S(1)} %fusion.52), custom_call_target="InvertDiagBlocksLowerTriangular" | custom-call | tf_op jit(solution)/shard_map/jit(_cho_solve)/triangular_solve | solution.py:97
  79.9 1.5 reshape.153
  81.5 1.9 dot_general.107
  83.4 1.6 multiply_reduce_fusion.5
  85.0 1.0 convolution_bitcast_fusion.3
  85.9 25.9 %psum.101 = f32[64,32]{0,1:T(8,128)S(1)} all-reduce(f32[64,32]{0,1:T(8,128)S(1)} %convolution_bitcast_fusion.3), channel_id=1, replica_groups=mesh['parts'=2,'slab'=4,'orb'=2,'pen'=2] {'slab','pen'}, use_global_device_ids=true, to_apply=%region_6.8 | all-reduce | flops 2048 | bytes 16384 | tf_op jit(solution)/shard_map/psum | solution.py:120
  112.2 1.4 multiply_reduce_fusion.3
  115.5 1.1 fusion.93
  116.6 3.8 %collective-permute-start = (f32[32,1,4,256]{3,0,2,1:T(8,128)}, f32[32,1,4,256]{3,0,2,1:T(8,128)}, u32[]{:S(2)}, u32[]{:S(2)}) collective-permute-start(f32[32,1,4,256]{3,0,2,1:T(8,128)} %get-tuple-element.45), channel_id=1, source_target_pairs={{4,0},{8,4},{12,8},{0,12},{5,1},{9,5},{13,9},{1,13},{6,2},{10,6},{... | collective-permute-start | bytes 393224 | tf_op jit(solution)/shard_map/ppermute | solution.py:21
  120.5 0.9 copy-done.2
  122.1 25.9 %psum.102 = f32[128,32]{0,1:T(8,128)S(1)} all-reduce(f32[128,32]{0,1:T(8,128)S(1)} %multiply_reduce_fusion.9), channel_id=1, replica_groups=mesh['parts'=2,'slab'=4,'orb'=2,'pen'=2] {'slab','pen'}, use_global_device_ids=true, to_apply=%region_8.10 | all-reduce | flops 4096 | bytes 32768 | tf_op jit(solution)/shard_map/psum | solution.py:44
  148.1 0.9 pad_maximum_fusion.43
  151.5 2.2 multiply_reduce_fusion.4
  155.6 1.2 fusion.90
  156.8 3.8 %collective-permute-start.4 = (f32[32,1,4,256]{3,0,2,1:T(8,128)}, f32[32,1,4,256]{3,0,2,1:T(8,128)}, u32[]{:S(2)}, u32[]{:S(2)}) collective-permute-start(f32[32,1,4,256]{3,0,2,1:T(8,128)} %get-tuple-element.39), channel_id=1, source_target_pairs={{4,0},{8,4},{12,8},{0,12},{5,1},{9,5},{13,9},{1,13},{6,2},{10,6},{... | collective-permute-start | bytes 393224 | tf_op jit(solution)/shard_map/ppermute | solution.py:21
  160.7 0.9 copy-done.3
  162.3 25.9 %psum.104 = f32[128,32]{0,1:T(8,128)S(1)} all-reduce(f32[128,32]{0,1:T(8,128)S(1)} %multiply_reduce_fusion.8), channel_id=1, replica_groups=mesh['parts'=2,'slab'=4,'orb'=2,'pen'=2] {'slab','pen'}, use_global_device_ids=true, to_apply=%region_12.14 | all-reduce | flops 4096 | bytes 32768 | tf_op jit(solution)/shard_map/psum | solution.py:44
  188.3 1.1 pad_maximum_fusion.40
  190.0 0.9 collective-permute-done.6
  191.2 2.3 fusion.6
  193.5 1.0 convolution_bitcast_fusion.2
  194.5 26.0 %all-reduce = (f32[64,32]{0,1:T(8,128)S(1)}, f32[32]{0:T(128)S(1)}, f32[32]{0:T(128)S(1)}) all-reduce(f32[64,32]{0,1:T(8,128)S(1)} %convolution_bitcast_fusion.2, f32[32]{0:T(128)S(1)} %get-tuple-element.46, f32[32]{0:T(128)S(1)} %multiply_add_fusion.3), channel_id=1, replica_groups=mesh['parts'=2,'slab'=4,'orb'=2,'pen'=2] {'slab','pen'}, use_global_device_ids=true, to_apply=%region_13.15 | all-reduce | flops 2112 | bytes 16896 | tf_op jit(solution)/shard_map/psum | solution.py:129
  220.9 2.5 multiply_reduce_fusion.2
  223.3 13.6 %psum.106 = f32[32]{0:T(128)S(1)} all-reduce(f32[32]{0:T(128)S(1)} %get-tuple-element.52), channel_id=1, replica_groups=mesh['parts'=2,'slab'=4,'orb'=2,'pen'=2] {'slab','pen'}, use_global_device_ids=true, to_apply=%region_15.17 | all-reduce | flops 32 | bytes 256 | tf_op jit(solution)/shard_map/psum | solution.py:104
  236.9 1.0 convolution_bitcast_fusion.1
  237.9 25.9 %psum.107 = f32[64,32]{0,1:T(8,128)S(1)} all-reduce(f32[64,32]{0,1:T(8,128)S(1)} %convolution_bitcast_fusion.1), channel_id=1, replica_groups=mesh['parts'=2,'slab'=4,'orb'=2,'pen'=2] {'slab','pen'}, use_global_device_ids=true, to_apply=%region_16.18 | all-reduce | flops 2048 | bytes 16384 | tf_op jit(solution)/shard_map/psum | solution.py:120
  264.2 1.4 multiply_reduce_fusion.1
  267.5 1.1 fusion.87
  268.6 3.8 %collective-permute-start.8 = (f32[32,1,4,256]{3,0,2,1:T(8,128)}, f32[32,1,4,256]{3,0,2,1:T(8,128)}, u32[]{:S(2)}, u32[]{:S(2)}) collective-permute-start(f32[32,1,4,256]{3,0,2,1:T(8,128)} %get-tuple-element.33), channel_id=1, source_target_pairs={{4,0},{8,4},{12,8},{0,12},{5,1},{9,5},{13,9},{1,13},{6,2},{10,6},{... | collective-permute-start | bytes 393224 | tf_op jit(solution)/shard_map/ppermute | solution.py:21
  272.6 0.9 copy-done.4
  274.1 26.1 %psum.108 = f32[128,32]{0,1:T(8,128)S(1)} all-reduce(f32[128,32]{0,1:T(8,128)S(1)} %multiply_reduce_fusion.7), channel_id=1, replica_groups=mesh['parts'=2,'slab'=4,'orb'=2,'pen'=2] {'slab','pen'}, use_global_device_ids=true, to_apply=%region_17.19 | all-reduce | flops 4096 | bytes 32768 | tf_op jit(solution)/shard_map/psum | solution.py:44
  300.3 0.9 pad_maximum_fusion.37
  301.8 0.9 collective-permute-done.10
  303.0 2.2 fusion.8
  305.2 13.8 %psum.109 = f32[32]{0:T(128)S(1)} all-reduce(f32[32]{0:T(128)S(1)} %multiply_add_fusion.2), channel_id=1, replica_groups=mesh['parts'=2,'slab'=4,'orb'=2,'pen'=2] {'slab','pen'}, use_global_device_ids=true, to_apply=%region_20.22 | all-reduce | flops 32 | bytes 256 | tf_op jit(solution)/shard_map/psum | solution.py:129
  321.4 3.8 %collective-permute-start.12 = (f32[32,1,4,256]{3,0,2,1:T(8,128)}, f32[32,1,4,256]{3,0,2,1:T(8,128)}, u32[]{:S(2)}, u32[]{:S(2)}) collective-permute-start(f32[32,1,4,256]{3,0,2,1:T(8,128)} %get-tuple-element.27), channel_id=1, source_target_pairs={{4,0},{8,4},{12,8},{0,12},{5,1},{9,5},{13,9},{1,13},{6,2},{10,6},{... | collective-permute-start | bytes 393224 | tf_op jit(solution)/shard_map/ppermute | solution.py:21
  326.0 25.9 %psum.110 = f32[128,32]{0,1:T(8,128)S(1)} all-reduce(f32[128,32]{0,1:T(8,128)S(1)} %multiply_reduce_fusion.6), channel_id=1, replica_groups=mesh['parts'=2,'slab'=4,'orb'=2,'pen'=2] {'slab','pen'}, use_global_device_ids=true, to_apply=%region_21.23 | all-reduce | flops 4096 | bytes 32768 | tf_op jit(solution)/shard_map/psum | solution.py:44
  353.4 0.9 collective-permute-done.14
  354.6 2.1 multiply_reduce_fusion
  356.7 7.2 %psum.111 = f32[4,4,256]{2,1,0:T(4,128)S(1)} all-reduce(f32[4,4,256]{2,1,0:T(4,128)S(1)} %get-tuple-element.56), channel_id=1, replica_groups=mesh['parts'=2,'slab'=4,'orb'=2,'pen'=2] {'orb'}, use_global_device_ids=true, to_apply=%region_23.25 | all-reduce | flops 4096 | bytes 32768 | tf_op jit(solution)/shard_map/psum | solution.py:142
  364.5 1.1 copy.59
  (132 shorter events, 22.3 us)
Async XLA Ops:
  7.2 27.0 %all-gather.2.cloned.1.call-start = ((), (), s32[]{:S(2)}) async-start(), calls=%async_computation | async-start | bytes 1572864 | tf_op jit(solution)/shard_map/all_gather | solution.py:88
  9.4 1.1 copy-start.10
  10.5 1.0 copy-start.1
  10.5 1.0 copy-start.21
  11.6 0.7 copy-start.20
  12.3 24.4 %copy-start.7 = (f32[32,4,4,256]{3,2,1,0:T(4,128)S(1)}, f32[32,4,4,256]{3,2,1,0:T(4,128)}, u32[]{:S(2)}) copy-start(f32[32,4,4,256]{3,2,1,0:T(4,128)} %param.11) | copy-start | bytes 1572868
  12.3 24.4 %copy-start.18 = (f32[4,4,256]{2,1,0:T(4,128)S(1)}, f32[4,4,256]{2,1,0:T(4,128)}, u32[]{:S(2)}) copy-start(f32[4,4,256]{2,1,0:T(4,128)} %param.15) | copy-start | bytes 49156
  34.1 2.6 copy-start
  116.6 31.5 %collective-permute-start.1 = (f32[32,1,4,256]{3,0,2,1:T(8,128)}, f32[32,1,4,256]{3,0,2,1:T(8,128)}, u32[]{:S(2)}, u32[]{:S(2)}) collective-permute-start(f32[32,1,4,256]{3,0,2,1:T(8,128)} %get-tuple-element.44), channel_id=1, source_target_pairs={{0,4},{4,8},{8,12},{12,0},{1,5},{5,9},{9,13},{13,1},{2,6},{6,10},{... | collective-permute-start | bytes 393224 | tf_op jit(solution)/shard_map/ppermute | solution.py:19
  116.6 31.5 %collective-permute-start = (f32[32,1,4,256]{3,0,2,1:T(8,128)}, f32[32,1,4,256]{3,0,2,1:T(8,128)}, u32[]{:S(2)}, u32[]{:S(2)}) collective-permute-start(f32[32,1,4,256]{3,0,2,1:T(8,128)} %get-tuple-element.45), channel_id=1, source_target_pairs={{4,0},{8,4},{12,8},{0,12},{5,1},{9,5},{13,9},{1,13},{6,2},{10,6},{... | collective-permute-start | bytes 393224 | tf_op jit(solution)/shard_map/ppermute | solution.py:21
  120.4 1.0 copy-start.2
  122.1 25.9 %copy-start.19 = (f32[128]{0:T(128)S(1)}, f32[128]{0:T(128)}, u32[]{:S(2)}) copy-start(f32[128]{0:T(128)} %param.18) | copy-start | bytes 1540
  148.1 2.8 copy-start.11
  148.1 2.7 copy-start.14
  149.0 1.5 collective-permute-start.2
  149.1 1.7 copy-start.22
  149.1 1.7 collective-permute-start.3
  150.8 0.7 copy-start.23
  153.6 2.0 copy-start.5
  156.8 31.5 %collective-permute-start.5 = (f32[32,1,4,256]{3,0,2,1:T(8,128)}, f32[32,1,4,256]{3,0,2,1:T(8,128)}, u32[]{:S(2)}, u32[]{:S(2)}) collective-permute-start(f32[32,1,4,256]{3,0,2,1:T(8,128)} %get-tuple-element.38), channel_id=1, source_target_pairs={{0,4},{4,8},{8,12},{12,0},{1,5},{5,9},{9,13},{13,1},{2,6},{6,10},{... | collective-permute-start | bytes 393224 | tf_op jit(solution)/shard_map/ppermute | solution.py:19
  156.8 31.5 %collective-permute-start.4 = (f32[32,1,4,256]{3,0,2,1:T(8,128)}, f32[32,1,4,256]{3,0,2,1:T(8,128)}, u32[]{:S(2)}, u32[]{:S(2)}) collective-permute-start(f32[32,1,4,256]{3,0,2,1:T(8,128)} %get-tuple-element.39), channel_id=1, source_target_pairs={{4,0},{8,4},{12,8},{0,12},{5,1},{9,5},{13,9},{1,13},{6,2},{10,6},{... | collective-permute-start | bytes 393224 | tf_op jit(solution)/shard_map/ppermute | solution.py:21
  160.6 1.0 copy-start.3
  188.2 3.0 copy-start.16
  188.2 3.0 copy-start.6
  188.2 3.0 copy-start.12
  189.4 1.5 collective-permute-start.6
  189.5 1.7 collective-permute-start.7
  193.5 1.0 copy-start.9
  268.6 31.6 %collective-permute-start.9 = (f32[32,1,4,256]{3,0,2,1:T(8,128)}, f32[32,1,4,256]{3,0,2,1:T(8,128)}, u32[]{:S(2)}, u32[]{:S(2)}) collective-permute-start(f32[32,1,4,256]{3,0,2,1:T(8,128)} %get-tuple-element.32), channel_id=1, source_target_pairs={{0,4},{4,8},{8,12},{12,0},{1,5},{5,9},{9,13},{13,1},{2,6},{6,10},{... | collective-permute-start | bytes 393224 | tf_op jit(solution)/shard_map/ppermute | solution.py:19
  268.6 31.7 %collective-permute-start.8 = (f32[32,1,4,256]{3,0,2,1:T(8,128)}, f32[32,1,4,256]{3,0,2,1:T(8,128)}, u32[]{:S(2)}, u32[]{:S(2)}) collective-permute-start(f32[32,1,4,256]{3,0,2,1:T(8,128)} %get-tuple-element.33), channel_id=1, source_target_pairs={{4,0},{8,4},{12,8},{0,12},{5,1},{9,5},{13,9},{1,13},{6,2},{10,6},{... | collective-permute-start | bytes 393224 | tf_op jit(solution)/shard_map/ppermute | solution.py:21
  272.5 1.0 copy-start.4
  300.3 2.7 copy-start.13
  300.3 2.7 copy-start.15
  301.2 1.5 collective-permute-start.10
  301.3 1.7 collective-permute-start.11
  321.4 30.5 %collective-permute-start.13 = (f32[32,1,4,256]{3,0,2,1:T(8,128)}, f32[32,1,4,256]{3,0,2,1:T(8,128)}, u32[]{:S(2)}, u32[]{:S(2)}) collective-permute-start(f32[32,1,4,256]{3,0,2,1:T(8,128)} %get-tuple-element.26), channel_id=1, source_target_pairs={{0,4},{4,8},{8,12},{12,0},{1,5},{5,9},{9,13},{13,1},{2,6},{6,10},{... | collective-permute-start | bytes 393224 | tf_op jit(solution)/shard_map/ppermute | solution.py:19
  321.4 30.5 %collective-permute-start.12 = (f32[32,1,4,256]{3,0,2,1:T(8,128)}, f32[32,1,4,256]{3,0,2,1:T(8,128)}, u32[]{:S(2)}, u32[]{:S(2)}) collective-permute-start(f32[32,1,4,256]{3,0,2,1:T(8,128)} %get-tuple-element.27), channel_id=1, source_target_pairs={{4,0},{8,4},{12,8},{0,12},{5,1},{9,5},{13,9},{1,13},{6,2},{10,6},{... | collective-permute-start | bytes 393224 | tf_op jit(solution)/shard_map/ppermute | solution.py:21
  351.9 2.7 copy-start.8
  351.9 2.7 copy-start.17
  352.8 1.5 collective-permute-start.14
  352.9 1.7 collective-permute-start.15
Sparse Core Ops, SparseCore 0:
  10.1 23.9 all-gather.1
where the time goes:
time: 373 us; the launch traced here: 372 us
  blocking collectives  245 us (66%)
  waiting for transfers between devices  26.6 us (7%)
  matrix products  25.8 us (7%)
  local copies, waits for them, and re-layouts  24.9 us (7%)
  starting transfers between devices  17.6 us (5%)
  other arithmetic  17.1 us (5%)
  between operations  15.3 us (4%)
    psum x4, blocking collectives, coefficients(): summed = lax.psum(partial_sum, ('slab', 'pen'))  104 us
    psum x2, blocking collectives, on_device(): direction_total = lax.psum(correlation_terms(direction), ('slab', 'pen'))  51.8 us
    psum x2, blocking collectives, on_device(): lax.psum((correlation_terms(target), curve_part), ('slab', 'pen'))  39.8 us
    psum x1, blocking collectives, on_device(): lax.psum((gram_part, correlation_terms(source)), ('slab', 'pen'))  28.8 us
    all_gather x1, waiting for transfers between devices, on_device(): everyone = lax.all_gather(orbitals, 'orb', axis=0, tiled=True)  21.8 us
    ppermute x8, starting transfers between devices, extended(): lax.ppermute(head, axis, [((i + 1) % count, i) for i in range(count)])  15.6 us
    psum x1, blocking collectives, squares(): return lax.psum(jnp.sum(values * values, axis=(1, 2, 3)), ('slab', 'pen'))  13.6 us
    dot_general x4, matrix products, apply_section(): lax.dot_general(flat_spread, flat_beta, (((0,), (0,)), ((), ())), precisi...  8.76 us
  transfers between devices with their start and end apart: 17, of which 9 were waited for; matrix products, arithmetic and copies ran while one was open for 1% of the time, Pallas kernels for 0%

commit v1 on v0

--- a/solution.py
+++ b/solution.py
@@ -41,7 +41,7 @@
     )
     inner_sums = inner_sums.reshape(projectors.shape[0], orb_count, plane_count)
     partial_sum = jnp.einsum("aiz,az->ai", inner_sums, weights, precision=highest)
-    summed = lax.psum(partial_sum, ("slab", "pen"))
+    summed = jnp.sum(lax.all_gather(partial_sum, ("slab", "pen")), axis=0)
     return couplings[:, None] * summed
 
 

time: 373 us -> 312 us (0.84)
  blocking collectives: 245 us -> 198 us
  local copies, waits for them, and re-layouts: 24.9 us -> 14.2 us
    psum x4 -> x0, blocking collectives: 104 us -> none  [coefficients(): summed = lax.psum(partial_sum, ('slab', 'pen'))]
    all_gather x0 -> x4, blocking collectives: none -> 56.1 us  [coefficients(): summed = jnp.sum(lax.all_gather(partial_sum, ('slab', 'pen')), axis=0)]
    slice x8, local copies, waits for them, and re-layouts: 7.01 us -> 1.38 us  [apply_section(): beside_all = beside_all + jnp.roll(centre, 1, 3) + jnp.roll(centre, -1, 3)]
    dot_general x4, matrix products: 8.76 us -> 4.56 us  [apply_section(): lax.dot_general(flat_spread, flat_beta, (((0,), (0,)), ((), ())), precisi...]
    slice x4, other arithmetic: 3.87 us -> 0.11 us  [extended(): head = lax.slice_in_dim(cells, 0, width, axis=dim)]
    unnamed x55 -> x39, local copies, waits for them, and re-layouts: 8.29 us -> 6.13 us
where the time goes in v1:
time: 312 us; the launch traced here: 311 us
  blocking collectives  198 us (63%)
  waiting for transfers between devices  26.9 us (9%)
  matrix products  25.6 us (8%)
  starting transfers between devices  18 us (6%)
  between operations  15.4 us (5%)
  local copies, waits for them, and re-layouts  14.2 us (5%)
  other arithmetic  13.5 us (4%)
    all_gather x4, blocking collectives, coefficients(): summed = jnp.sum(lax.all_gather(partial_sum, ('slab', 'pen')), axis=0)  56.1 us
    psum x2, blocking collectives, on_device(): direction_total = lax.psum(correlation_terms(direction), ('slab', 'pen'))  51.8 us
    psum x2, blocking collectives, on_device(): lax.psum((correlation_terms(target), curve_part), ('slab', 'pen'))  40.2 us
    psum x1, blocking collectives, on_device(): lax.psum((gram_part, correlation_terms(source)), ('slab', 'pen'))  28.8 us
    all_gather x1, waiting for transfers between devices, on_device(): everyone = lax.all_gather(orbitals, 'orb', axis=0, tiled=True)  21.8 us
    ppermute x8, starting transfers between devices, extended(): lax.ppermute(head, axis, [((i + 1) % count, i) for i in range(count)])  16.9 us
    psum x1, blocking collectives, squares(): return lax.psum(jnp.sum(values * values, axis=(1, 2, 3)), ('slab', 'pen'))  13.6 us
    dot_general x4, matrix products, removed(): lax.dot_general(expansion, every_flat, (((0,), (0,)), ((), ())), precisio...  9.74 us
  transfers between devices with their start and end apart: 17, of which 9 were waited for; matrix products, arithmetic and copies ran while one was open for 1% of the time, Pallas kernels for 0%

profile of v1, /device:TPU:0, one launch (start us, length us, event | category | flops | bytes accessed | tf_op | source)
XLA Modules:
  0.0 311.3 jit_solution(11323838430378516785)
XLA Ops:
  7.2 2.1 copy.60
  10.5 1.0 copy.69
  11.6 0.6 copy-done.10
  12.3 21.8 %all-gather.6.cloned.1.call-done = f32[64,4,4,256]{3,0,2,1:T(8,128)} async-done(((f32[32,4,4,256]{3,0,2,1:T(8,128)}), f32[64,4,4,256]{3,0,2,1:T(8,128)}) %all-gather.6.cloned.1.call-update) | async-done | bytes 1048592 | tf_op jit(solution)/shard_map/all_gather | solution.py:88
  34.1 2.6 convolution_bitcast_fusion
  36.8 1.1 convolution_bitcast_fusion.4
  37.9 28.8 %all-reduce.1 = (f32[64,64]{0,1:T(8,128)S(1)}, f32[64,32]{0,1:T(8,128)S(1)}) all-reduce(f32[64,64]{0,1:T(8,128)S(1)} %convolution_bitcast_fusion, f32[64,32]{0,1:T(8,128)S(1)} %convolution_bitcast_fusion.4), channel_id=1, replica_groups=mesh['parts'=2,'slab'=4,'orb'=2,'pen'=2] {'slab','pen'}, use_global_device_ids=true, to_apply=%region_0.1 | all-reduce | flops 6144 | bytes 49152 | tf_op jit(solution)/shard_map/psum | solution.py:113
  66.8 5.8 %cholesky.18 = f32[64,64]{1,0:T(8,128)S(1)} custom-call(f32[64,64]{1,0:T(8,128)S(1)} %fusion.65), custom_call_target="Cholesky" | custom-call | tf_op jit(solution)/shard_map/jit(cholesky)/cholesky | solution.py:114
  72.7 0.6 compare_reduce_fusion
  73.4 0.7 fusion.52
  74.0 4.9 %custom-call.11 = f32[1,64,64]{1,2,0:T(8,128)S(1)} custom-call(f32[1,64,64]{2,1,0:T(8,128)S(1)} %fusion.52), custom_call_target="InvertDiagBlocksLowerTriangular" | custom-call | tf_op jit(solution)/shard_map/jit(_cho_solve)/triangular_solve | solution.py:97
  79.3 0.7 copy.64
  79.9 1.5 reshape.214
  81.5 1.9 dot_general.107
  83.4 2.6 multiply_reduce_fusion.5
  86.0 1.0 convolution_bitcast_fusion.3
  87.0 25.9 %psum.73 = f32[64,32]{0,1:T(8,128)S(1)} all-reduce(f32[64,32]{0,1:T(8,128)S(1)} %convolution_bitcast_fusion.3), channel_id=1, replica_groups=mesh['parts'=2,'slab'=4,'orb'=2,'pen'=2] {'slab','pen'}, use_global_device_ids=true, to_apply=%region_6.8 | all-reduce | flops 2048 | bytes 16384 | tf_op jit(solution)/shard_map/psum | solution.py:120
  113.2 1.4 multiply_reduce_fusion.3
  115.6 3.8 %collective-permute-start = (f32[32,1,4,256]{3,0,2,1:T(8,128)S(1)}, f32[32,1,4,256]{3,0,2,1:T(8,128)S(1)}, u32[]{:S(2)}, u32[]{:S(2)}) collective-permute-start(f32[32,1,4,256]{3,0,2,1:T(8,128)S(1)} %get-tuple-element.47), channel_id=1, source_target_pairs={{4,0},{8,4},{12,8},{0,12},{5,1},{9,5},{13,9},{1,13},{6,2},{10,6},{... | collective-permute-start | bytes 393224 | tf_op jit(solution)/shard_map/ppermute | solution.py:21
  120.2 14.0 %all-gather = f32[1024,32]{0,1:T(8,128)S(1)} all-gather(f32[128,32]{0,1:T(8,128)S(1)} %multiply_reduce_fusion.9), channel_id=2, replica_groups=mesh['parts'=2,'slab'=4,'orb'=2,'pen'=2] {'slab','pen'}, dimensions={0}, use_global_device_ids=true | all-gather | bytes 147456 | tf_op jit(solution)/shard_map/all_gather | solution.py:44
  134.2 0.6 copy-done.9
  135.5 0.9 collective-permute-done.2
  136.8 0.6 copy-done.13
  137.4 1.2 multiply_reduce_fusion.4
  139.4 3.8 %collective-permute-start.4 = (f32[32,1,4,256]{3,0,2,1:T(8,128)S(1)}, f32[32,1,4,256]{3,0,2,1:T(8,128)S(1)}, u32[]{:S(2)}, u32[]{:S(2)}) collective-permute-start(f32[32,1,4,256]{3,0,2,1:T(8,128)S(1)} %get-tuple-element.41), channel_id=1, source_target_pairs={{4,0},{8,4},{12,8},{0,12},{5,1},{9,5},{13,9},{1,13},{6,2},{10,6},{... | collective-permute-start | bytes 393224 | tf_op jit(solution)/shard_map/ppermute | solution.py:21
  143.9 14.0 %all-gather.1 = f32[1024,32]{0,1:T(8,128)S(1)} all-gather(f32[128,32]{0,1:T(8,128)S(1)} %multiply_reduce_fusion.8), channel_id=3, replica_groups=mesh['parts'=2,'slab'=4,'orb'=2,'pen'=2] {'slab','pen'}, dimensions={0}, use_global_device_ids=true | all-gather | bytes 147456 | tf_op jit(solution)/shard_map/all_gather | solution.py:44
  158.6 0.9 collective-permute-done.6
  159.9 1.1 fusion.6
  161.0 1.0 convolution_bitcast_fusion.2
  162.0 26.3 %all-reduce = (f32[64,32]{0,1:T(8,128)S(1)}, f32[32]{0:T(128)S(1)}, f32[32]{0:T(128)S(1)}) all-reduce(f32[64,32]{0,1:T(8,128)S(1)} %convolution_bitcast_fusion.2, f32[32]{0:T(128)S(1)} %get-tuple-element.48, f32[32]{0:T(128)S(1)} %multiply_add_fusion.3), channel_id=1, replica_groups=mesh['parts'=2,'slab'=4,'orb'=2,'pen'=2] {'slab','pen'}, use_global_device_ids=true, to_apply=%region_13.15 | all-reduce | flops 2112 | bytes 16896 | tf_op jit(solution)/shard_map/psum | solution.py:129
  188.6 3.3 %multiply_reduce_fusion.2 = (f32[32]{0:T(128)S(1)}, f32[32,4,4,256]{3,0,2,1:T(8,128)}) fusion(f32[32,4,4,256]{3,0,2,1:T(8,128)} %copy-done.4, f32[64,32,1,1]{0,1,3,2:T(8,128)S(1)} %convolution_bitcast_fusion.6, f32[4,4,256,64]{2,1,0,3:T(4,128)S(1)} %dot_general.107, f32[32]{0:T(128)S(1)} %div.41, f32[32,4,4,256]{3,0,2,1:T(8,128)S(1)} %get-tuple-element.49), kind=kOutput, calls=%fused_computation.98 | convolution fusion | flops 101449696 | bytes 2629888 | tf_op jit(solution)/shard_map/dot_general | solution.py:98
  191.9 13.6 %psum.76 = f32[32]{0:T(128)S(1)} all-reduce(f32[32]{0:T(128)S(1)} %get-tuple-element.54), channel_id=1, replica_groups=mesh['parts'=2,'slab'=4,'orb'=2,'pen'=2] {'slab','pen'}, use_global_device_ids=true, to_apply=%region_15.17 | all-reduce | flops 32 | bytes 256 | tf_op jit(solution)/shard_map/psum | solution.py:104
  205.5 2.0 convolution_bitcast_fusion.1
  207.5 25.9 %psum.77 = f32[64,32]{0,1:T(8,128)S(1)} all-reduce(f32[64,32]{0,1:T(8,128)S(1)} %convolution_bitcast_fusion.1), channel_id=1, replica_groups=mesh['parts'=2,'slab'=4,'orb'=2,'pen'=2] {'slab','pen'}, use_global_device_ids=true, to_apply=%region_16.18 | all-reduce | flops 2048 | bytes 16384 | tf_op jit(solution)/shard_map/psum | solution.py:120
  233.7 2.5 multiply_reduce_fusion.1
  237.0 3.8 %collective-permute-start.8 = (f32[32,1,4,256]{3,0,2,1:T(8,128)S(1)}, f32[32,1,4,256]{3,0,2,1:T(8,128)S(1)}, u32[]{:S(2)}, u32[]{:S(2)}) collective-permute-start(f32[32,1,4,256]{3,0,2,1:T(8,128)S(1)} %get-tuple-element.35), channel_id=1, source_target_pairs={{4,0},{8,4},{12,8},{0,12},{5,1},{9,5},{13,9},{1,13},{6,2},{10,6},{... | collective-permute-start | bytes 393224 | tf_op jit(solution)/shard_map/ppermute | solution.py:21
  241.6 14.2 %all-gather.2 = f32[1024,32]{0,1:T(8,128)S(1)} all-gather(f32[128,32]{0,1:T(8,128)S(1)} %multiply_reduce_fusion.7), channel_id=4, replica_groups=mesh['parts'=2,'slab'=4,'orb'=2,'pen'=2] {'slab','pen'}, dimensions={0}, use_global_device_ids=true | all-gather | bytes 147456 | tf_op jit(solution)/shard_map/all_gather | solution.py:44
  256.5 0.9 collective-permute-done.10
  257.8 1.0 fusion.8
  258.8 13.9 %psum.78 = f32[32]{0:T(128)S(1)} all-reduce(f32[32]{0:T(128)S(1)} %multiply_add_fusion.2), channel_id=1, replica_groups=mesh['parts'=2,'slab'=4,'orb'=2,'pen'=2] {'slab','pen'}, use_global_device_ids=true, to_apply=%region_20.22 | all-reduce | flops 32 | bytes 256 | tf_op jit(solution)/shard_map/psum | solution.py:129
  273.7 3.8 %collective-permute-start.12 = (f32[32,1,4,256]{3,0,2,1:T(8,128)S(1)}, f32[32,1,4,256]{3,0,2,1:T(8,128)S(1)}, u32[]{:S(2)}, u32[]{:S(2)}) collective-permute-start(f32[32,1,4,256]{3,0,2,1:T(8,128)S(1)} %get-tuple-element.29), channel_id=1, source_target_pairs={{4,0},{8,4},{12,8},{0,12},{5,1},{9,5},{13,9},{1,13},{6,2},{10,6},{... | collective-permute-start | bytes 393224 | tf_op jit(solution)/shard_map/ppermute | solution.py:21
  277.6 0.6 fusion.99
  278.2 14.0 %all-gather.3 = f32[1024,32]{0,1:T(8,128)S(1)} all-gather(f32[128,32]{0,1:T(8,128)S(1)} %multiply_reduce_fusion.6), channel_id=5, replica_groups=mesh['parts'=2,'slab'=4,'orb'=2,'pen'=2] {'slab','pen'}, dimensions={0}, use_global_device_ids=true | all-gather | bytes 147456 | tf_op jit(solution)/shard_map/all_gather | solution.py:44
  293.0 0.9 collective-permute-done.14
  294.2 1.3 multiply_reduce_fusion
  295.5 7.2 %psum.79 = f32[4,4,256]{2,1,0:T(4,128)S(1)} all-reduce(f32[4,4,256]{2,1,0:T(4,128)S(1)} %get-tuple-element.58), channel_id=1, replica_groups=mesh['parts'=2,'slab'=4,'orb'=2,'pen'=2] {'orb'}, use_global_device_ids=true, to_apply=%region_23.25 | all-reduce | flops 4096 | bytes 32768 | tf_op jit(solution)/shard_map/psum | solution.py:142
  302.8 0.6 broadcast_multiply_fusion.1
  303.4 1.1 copy.83
  (120 shorter events, 11.9 us)
Async XLA Ops:
  7.2 27.0 %all-gather.6.cloned.1.call-start = ((), (), s32[]{:S(2)}) async-start(), calls=%async_computation | async-start | bytes 1572864 | tf_op jit(solution)/shard_map/all_gather | solution.py:88
  9.4 1.1 copy-start.5
  10.5 1.0 copy-start.11
  11.5 0.7 copy-start.10
  12.3 24.4 %copy-start.2 = (f32[32,4,4,256]{3,2,1,0:T(4,128)S(1)}, f32[32,4,4,256]{3,2,1,0:T(4,128)}, u32[]{:S(2)}) copy-start(f32[32,4,4,256]{3,2,1,0:T(4,128)} %param.11) | copy-start | bytes 1572868
  12.3 24.5 %copy-start.8 = (f32[4,4,256]{2,1,0:T(4,128)S(1)}, f32[4,4,256]{2,1,0:T(4,128)}, u32[]{:S(2)}) copy-start(f32[4,4,256]{2,1,0:T(4,128)} %param.15) | copy-start | bytes 49156
  34.1 2.6 copy-start
  115.4 19.5 %collective-permute-start.1 = (f32[32,1,4,256]{3,0,2,1:T(8,128)S(1)}, f32[32,1,4,256]{3,0,2,1:T(8,128)S(1)}, u32[]{:S(2)}, u32[]{:S(2)}) collective-permute-start(f32[32,1,4,256]{3,0,2,1:T(8,128)S(1)} %get-tuple-element.46), channel_id=1, source_target_pairs={{0,4},{4,8},{8,12},{12,0},{1,5},{5,9},{9,13},{13,1},{2,6},{6,10},{... | collective-permute-start | bytes 393224 | tf_op jit(solution)/shard_map/ppermute | solution.py:19
  115.6 19.3 %collective-permute-start = (f32[32,1,4,256]{3,0,2,1:T(8,128)S(1)}, f32[32,1,4,256]{3,0,2,1:T(8,128)S(1)}, u32[]{:S(2)}, u32[]{:S(2)}) collective-permute-start(f32[32,1,4,256]{3,0,2,1:T(8,128)S(1)} %get-tuple-element.47), channel_id=1, source_target_pairs={{4,0},{8,4},{12,8},{0,12},{5,1},{9,5},{13,9},{1,13},{6,2},{10,6},{... | collective-permute-start | bytes 393224 | tf_op jit(solution)/shard_map/ppermute | solution.py:21
  134.2 0.7 copy-start.9
  134.8 1.9 copy-start.6
  134.9 1.5 collective-permute-start.2
  135.3 1.5 copy-start.12
  135.3 1.4 collective-permute-start.3
  136.8 0.7 copy-start.13
  139.3 18.7 %collective-permute-start.5 = (f32[32,1,4,256]{3,0,2,1:T(8,128)S(1)}, f32[32,1,4,256]{3,0,2,1:T(8,128)S(1)}, u32[]{:S(2)}, u32[]{:S(2)}) collective-permute-start(f32[32,1,4,256]{3,0,2,1:T(8,128)S(1)} %get-tuple-element.40), channel_id=1, source_target_pairs={{0,4},{4,8},{8,12},{12,0},{1,5},{5,9},{9,13},{13,1},{2,6},{6,10},{... | collective-permute-start | bytes 393224 | tf_op jit(solution)/shard_map/ppermute | solution.py:19
  139.4 18.6 %collective-permute-start.4 = (f32[32,1,4,256]{3,0,2,1:T(8,128)S(1)}, f32[32,1,4,256]{3,0,2,1:T(8,128)S(1)}, u32[]{:S(2)}, u32[]{:S(2)}) collective-permute-start(f32[32,1,4,256]{3,0,2,1:T(8,128)S(1)} %get-tuple-element.41), channel_id=1, source_target_pairs={{4,0},{8,4},{12,8},{0,12},{5,1},{9,5},{13,9},{1,13},{6,2},{10,6},{... | collective-permute-start | bytes 393224 | tf_op jit(solution)/shard_map/ppermute | solution.py:21
  158.0 1.5 collective-permute-start.6
  158.4 1.4 collective-permute-start.7
  161.0 1.0 copy-start.4
  236.9 18.9 %collective-permute-start.9 = (f32[32,1,4,256]{3,0,2,1:T(8,128)S(1)}, f32[32,1,4,256]{3,0,2,1:T(8,128)S(1)}, u32[]{:S(2)}, u32[]{:S(2)}) collective-permute-start(f32[32,1,4,256]{3,0,2,1:T(8,128)S(1)} %get-tuple-element.34), channel_id=1, source_target_pairs={{0,4},{4,8},{8,12},{12,0},{1,5},{5,9},{9,13},{13,1},{2,6},{6,10},{... | collective-permute-start | bytes 393224 | tf_op jit(solution)/shard_map/ppermute | solution.py:19
  237.0 18.8 %collective-permute-start.8 = (f32[32,1,4,256]{3,0,2,1:T(8,128)S(1)}, f32[32,1,4,256]{3,0,2,1:T(8,128)S(1)}, u32[]{:S(2)}, u32[]{:S(2)}) collective-permute-start(f32[32,1,4,256]{3,0,2,1:T(8,128)S(1)} %get-tuple-element.35), channel_id=1, source_target_pairs={{4,0},{8,4},{12,8},{0,12},{5,1},{9,5},{13,9},{1,13},{6,2},{10,6},{... | collective-permute-start | bytes 393224 | tf_op jit(solution)/shard_map/ppermute | solution.py:21
  255.8 1.9 copy-start.7
  255.9 1.5 collective-permute-start.10
  256.3 1.4 collective-permute-start.11
  257.8 14.9 %copy-start.1 = (f32[32,4,4,256]{3,0,2,1:T(8,128)S(1)}, f32[32,4,4,256]{3,0,2,1:T(8,128)}, u32[]{:S(2)}) copy-start(f32[32,4,4,256]{3,0,2,1:T(8,128)} %get-tuple-element.55) | copy-start | bytes 1572868
  273.6 18.7 %collective-permute-start.13 = (f32[32,1,4,256]{3,0,2,1:T(8,128)S(1)}, f32[32,1,4,256]{3,0,2,1:T(8,128)S(1)}, u32[]{:S(2)}, u32[]{:S(2)}) collective-permute-start(f32[32,1,4,256]{3,0,2,1:T(8,128)S(1)} %get-tuple-element.28), channel_id=1, source_target_pairs={{0,4},{4,8},{8,12},{12,0},{1,5},{5,9},{9,13},{13,1},{2,6},{6,10},{... | collective-permute-start | bytes 393224 | tf_op jit(solution)/shard_map/ppermute | solution.py:19
  273.7 18.7 %collective-permute-start.12 = (f32[32,1,4,256]{3,0,2,1:T(8,128)S(1)}, f32[32,1,4,256]{3,0,2,1:T(8,128)S(1)}, u32[]{:S(2)}, u32[]{:S(2)}) collective-permute-start(f32[32,1,4,256]{3,0,2,1:T(8,128)S(1)} %get-tuple-element.29), channel_id=1, source_target_pairs={{4,0},{8,4},{12,8},{0,12},{5,1},{9,5},{13,9},{1,13},{6,2},{10,6},{... | collective-permute-start | bytes 393224 | tf_op jit(solution)/shard_map/ppermute | solution.py:21
  292.3 1.9 copy-start.3
  292.4 1.5 collective-permute-start.14
  292.8 1.4 collective-permute-start.15
Sparse Core Ops, SparseCore 0:
  10.1 23.9 all-gather.5
